TPU v7x, 32 devices: a whole 2x2x4 slice. The times are simulated.
32 devices in a mesh: rows: 4 (over y, x), pairs: 8 (over z, core).
Axes of the slice: x: 2, y: 2, z: 4, core: 2. Of those that a mesh axis runs over, the one named last changes fastest.
Arguments:
- latent: bfloat16 [8192, 3072], P('rows', 'pairs'), as said below
Outputs:
- rotated_latent: bfloat16 [8192, 3072], P('rows', 'pairs')
Inputs may be any that keep to these rules, and one draw needn't show every extreme that they name: `latent`: finite real entries.
All inputs are finite; a program needn't handle non-finite values.
Results may differ from a plain program's by a relative error of at most 0.0065.
Values may be sent and summed in bfloat16 or wider, within the bound.
No kernel may reach another device: no remote copies, remote signals or barrier semaphores. Data moves between devices by JAX's collectives and lax.ppermute only.
A program may use at most 64 MiB of HBM per device.

v0:
```python
import math
import jax
import jax.numpy as jnp
from jax import lax
from jax.sharding import PartitionSpec as P

ROUNDS = 2
NS_ITERS = 2


def passed_along(shard, axis, by):
    peers = lax.axis_size(axis)
    return lax.ppermute(shard, axis, [(i, (i + by) % peers) for i in range(peers)])


def orthogonal(norms, cross):
    half = cross.shape[0]
    corr = cross / jnp.sqrt(norms[:half, None] * norms[None, half:])
    total = jnp.sqrt(2.0 * jnp.sum(corr * corr) + 1e-12)
    scaled = corr * (8.0 / total)
    empty = jnp.zeros((half, half), jnp.float32)
    upper = jnp.concatenate([empty, scaled], axis=1)
    lower = jnp.concatenate([-scaled.T, empty], axis=1)
    ident = jnp.eye(2 * half, dtype=jnp.float32)
    current = (ident + jnp.concatenate([upper, lower], axis=0)) * (1.5 / math.sqrt(65.0))
    for _ in range(NS_ITERS):
        inner = jnp.dot(current.T, current, precision=lax.Precision.HIGHEST)
        current = 1.5 * current - 0.5 * jnp.dot(current, inner, precision=lax.Precision.HIGHEST)
    return current.astype(jnp.bfloat16)


def rotor_of(window):
    half = window.shape[1] // 2
    gram = jnp.dot(window.T, window, preferred_element_type=jnp.float32)
    gram = lax.psum(gram, "rows")
    return orthogonal(jnp.diagonal(gram), gram[:half, half:])


def local(latent):
    half = latent.shape[1] // 2
    window = latent
    for _ in range(ROUNDS):
        from_below = passed_along(window, "pairs", 1)
        from_above = passed_along(window, "pairs", -1)
        rotor = rotor_of(window)
        left_rotor = passed_along(rotor[:, :half], "pairs", 1)
        right_rotor = passed_along(rotor[:, half:], "pairs", -1)
        left_next = jnp.dot(from_below, left_rotor, preferred_element_type=jnp.float32).astype(
            jnp.bfloat16
        )
        right_next = jnp.dot(from_above, right_rotor, preferred_element_type=jnp.float32).astype(
            jnp.bfloat16
        )
        window = jnp.concatenate([left_next, right_next], axis=1)
    return window


def solution(mesh):
    return jax.shard_map(
        local,
        mesh=mesh,
        in_specs=(P("rows", "pairs"),),
        out_specs=P("rows", "pairs"),
        check_vma=False,
    )
```

profile of v0, /device:TPU:0, one launch (start us, length us, event | category | flops | bytes accessed | tf_op | source)
XLA Modules:
  0.0 162.5 jit_solution(6450090133549089609)
XLA Ops:
  6.5 3.9 %fusion.51 = f32[384,384]{1,0:T(8,128)} fusion(bf16[2048,384]{1,0:T(8,128)(2,1)} %param.1), kind=kOutput, calls=%fused_computation.75 | convolution fusion | flops 603979776 | bytes 2162688 | tf_op jit(solution)/shard_map/dot_general | solution.py:34
  10.5 4.6 %collective-permute-start.3 = (bf16[2048,384]{1,0:T(8,128)(2,1)S(1)}, bf16[2048,384]{1,0:T(8,128)(2,1)}, u32[]{:S(2)}, u32[]{:S(2)}) collective-permute-start(bf16[2048,384]{1,0:T(8,128)(2,1)S(1)} %copy-done.2), channel_id=1, source_target_pairs={{0,7},{1,0},{2,1},{3,2},{4,3},{5,4},{6,5},{7,6},{8,15},{9,8},{10,9... | collective-permute-start | bytes 4718600 | tf_op jit(solution)/shard_map/ppermute | solution.py:13
  15.1 44.2 %all-reduce.7.cloned.1.call-done = f32[384,384]{1,0:T(8,128)} async-done(((f32[384,384]{1,0:T(8,128)}), f32[384,384]{1,0:T(8,128)}) %all-reduce.7.cloned.1.call-update) | async-done | bytes 589840 | tf_op jit(solution)/shard_map/psum | solution.py:35
  59.3 6.3 %gather_fusion = f32[384]{0:T(512)S(1)} fusion(f32[384,384]{1,0:T(8,128)} %all-reduce.7.cloned.1.call-done, s32[384]{0:T(512)S(1)} %or_reduce_fusion), kind=kCustom, calls=%fused_computation | custom fusion | bytes 6144 | tf_op jit(solution)/shard_map/jit(diagonal)/cond/branch_0_fun/gather | solution.py:36
  67.4 1.3 fusion.12
  68.7 1.4 fusion.2
  71.5 1.4 fusion.7
  72.9 2.6 %collective-permute-start.2 = (bf16[384,192]{0,1:T(8,128)(2,1)S(1)}, bf16[384,192]{0,1:T(8,128)(2,1)S(1)}, u32[]{:S(2)}, u32[]{:S(2)}) collective-permute-start(bf16[384,192]{0,1:T(8,128)(2,1)S(1)} %get-tuple-element.12), channel_id=1, source_target_pairs={{0,7},{1,0},{2,1},{3,2},{4,3},{5,4},{6,5},{7,6},{8,15},{9,8},{10,9... | collective-permute-start | bytes 442376 | tf_op jit(solution)/shard_map/ppermute | solution.py:13
  75.4 2.7 %collective-permute-done.2 = bf16[384,192]{0,1:T(8,128)(2,1)S(1)} collective-permute-done((bf16[384,192]{0,1:T(8,128)(2,1)S(1)}, bf16[384,192]{0,1:T(8,128)(2,1)S(1)}, u32[]{:S(2)}, u32[]{:S(2)}) %collective-permute-start.2) | collective-permute-done | bytes 147488 | tf_op jit(solution)/shard_map/ppermute | solution.py:13
  78.1 2.1 %fusion.1 = bf16[2048,192]{0,1:T(8,128)(2,1)S(1)} fusion(bf16[384,192]{0,1:T(8,128)(2,1)S(1)} %collective-permute-done.2, bf16[2048,384]{1,0:T(8,128)(2,1)} %collective-permute-done.3), kind=kOutput, calls=%fused_computation.7 | convolution fusion | flops 302383104 | bytes 2506752 | tf_op jit(solution)/shard_map/dot_general | solution.py:51
  80.3 1.5 collective-permute-done
  81.8 2.1 %fusion = bf16[2048,192]{0,1:T(8,128)(2,1)S(1)} fusion(bf16[384,192]{0,1:T(8,128)(2,1)S(1)} %collective-permute-done, bf16[2048,384]{1,0:T(8,128)(2,1)} %collective-permute-done.1), kind=kOutput, calls=%fused_computation.6 | convolution fusion | flops 302383104 | bytes 2506752 | tf_op jit(solution)/shard_map/dot_general | solution.py:48
  83.9 1.8 %fusion.44 = f32[384,384]{1,0:T(8,128)} fusion(bf16[2048,192]{0,1:T(8,128)(2,1)S(1)} %fusion.1, bf16[2048,192]{0,1:T(8,128)(2,1)S(1)} %fusion), kind=kOutput, calls=%fused_computation.70 | convolution fusion | flops 607125504 | bytes 2162688 | tf_op jit(solution)/shard_map/dot_general | solution.py:34
  87.0 2.2 %collective-permute-start.6 = (bf16[2048,384]{0,1:T(8,128)(2,1)}, bf16[2048,384]{0,1:T(8,128)(2,1)}, u32[]{:S(2)}, u32[]{:S(2)}) collective-permute-start(bf16[2048,384]{0,1:T(8,128)(2,1)} %pad_maximum_fusion), channel_id=1, source_target_pairs={{0,7},{1,0},{2,1},{3,2},{4,3},{5,4},{6,5},{7,6},{8,15},{9,8},{10,9... | collective-permute-start | bytes 4718600 | tf_op jit(solution)/shard_map/ppermute | solution.py:13
  89.3 41.6 %all-reduce.9.cloned.1.call-done = f32[384,384]{1,0:T(8,128)} async-done(((f32[384,384]{1,0:T(8,128)}), f32[384,384]{1,0:T(8,128)}) %all-reduce.9.cloned.1.call-update) | async-done | bytes 589840 | tf_op jit(solution)/shard_map/psum | solution.py:35
  130.9 6.3 %gather_fusion.1 = f32[384]{0:T(512)S(1)} fusion(f32[384,384]{1,0:T(8,128)} %all-reduce.9.cloned.1.call-done, s32[384]{0:T(512)S(1)} %or_reduce_fusion), kind=kCustom, calls=%fused_computation.1 | custom fusion | bytes 6144 | tf_op jit(solution)/shard_map/jit(diagonal)/cond/branch_0_fun/gather | solution.py:36
  139.0 1.3 fusion.9
  140.4 1.4 fusion.4
  143.1 1.3 fusion.6
  144.4 2.6 %collective-permute-start.7 = (bf16[384,192]{0,1:T(8,128)(2,1)S(1)}, bf16[384,192]{0,1:T(8,128)(2,1)S(1)}, u32[]{:S(2)}, u32[]{:S(2)}) collective-permute-start(bf16[384,192]{0,1:T(8,128)(2,1)S(1)} %get-tuple-element.10), channel_id=1, source_target_pairs={{0,7},{1,0},{2,1},{3,2},{4,3},{5,4},{6,5},{7,6},{8,15},{9,8},{10,9... | collective-permute-start | bytes 442376 | tf_op jit(solution)/shard_map/ppermute | solution.py:13
  147.0 2.7 %collective-permute-done.7 = bf16[384,192]{0,1:T(8,128)(2,1)S(1)} collective-permute-done((bf16[384,192]{0,1:T(8,128)(2,1)S(1)}, bf16[384,192]{0,1:T(8,128)(2,1)S(1)}, u32[]{:S(2)}, u32[]{:S(2)}) %collective-permute-start.7) | collective-permute-done | bytes 147488 | tf_op jit(solution)/shard_map/ppermute | solution.py:13
  149.7 2.0 %convolution_convert_fusion = bf16[2048,192]{0,1:T(8,128)(2,1)S(1)} fusion(bf16[384,192]{0,1:T(8,128)(2,1)S(1)} %collective-permute-done.7, bf16[2048,384]{0,1:T(8,128)(2,1)} %collective-permute-done.6), kind=kOutput, calls=%fused_computation.2 | convolution fusion | flops 302383104 | bytes 2506752 | tf_op jit(solution)/shard_map/dot_general | solution.py:51
  151.7 1.7 %collective-permute-done.5 = bf16[384,192]{0,1:T(8,128)(2,1)S(1)} collective-permute-done((bf16[384,192]{0,1:T(8,128)(2,1)S(1)}, bf16[384,192]{0,1:T(8,128)(2,1)S(1)}, u32[]{:S(2)}, u32[]{:S(2)}) %collective-permute-start.5) | collective-permute-done | bytes 147488 | tf_op jit(solution)/shard_map/ppermute | solution.py:13
  154.1 1.6 copy.7
  (34 shorter events, 6.9 us)
Async XLA Ops:
  6.5 4.0 %copy-start.2 = (bf16[2048,384]{1,0:T(8,128)(2,1)S(1)}, bf16[2048,384]{1,0:T(8,128)(2,1)}, u32[]{:S(2)}) copy-start(bf16[2048,384]{1,0:T(8,128)(2,1)} %param.1) | copy-start | bytes 4718596
  6.5 52.8 %all-reduce.7.cloned.1.call-start = ((), (), s32[]{:S(2)}) async-start(), calls=%async_computation | async-start | bytes 1179648 | tf_op jit(solution)/shard_map/psum | solution.py:35
  10.5 120.4 %all-reduce.9.cloned.1.call-start = ((), (), s32[]{:S(2)}) async-start(), calls=%async_computation.1 | async-start | bytes 1179648 | tf_op jit(solution)/shard_map/psum | solution.py:35
  10.5 67.6 %collective-permute-start.3 = (bf16[2048,384]{1,0:T(8,128)(2,1)S(1)}, bf16[2048,384]{1,0:T(8,128)(2,1)}, u32[]{:S(2)}, u32[]{:S(2)}) collective-permute-start(bf16[2048,384]{1,0:T(8,128)(2,1)S(1)} %copy-done.2), channel_id=1, source_target_pairs={{0,7},{1,0},{2,1},{3,2},{4,3},{5,4},{6,5},{7,6},{8,15},{9,8},{10,9... | collective-permute-start | bytes 4718600 | tf_op jit(solution)/shard_map/ppermute | solution.py:13
  15.1 66.7 %collective-permute-start.1 = (bf16[2048,384]{1,0:T(8,128)(2,1)S(1)}, bf16[2048,384]{1,0:T(8,128)(2,1)}, u32[]{:S(2)}, u32[]{:S(2)}) collective-permute-start(bf16[2048,384]{1,0:T(8,128)(2,1)S(1)} %copy-done.2), channel_id=1, source_target_pairs={{0,1},{1,2},{2,3},{3,4},{4,5},{5,6},{6,7},{7,0},{8,9},{9,10},{10,1... | collective-permute-start | bytes 4718600 | tf_op jit(solution)/shard_map/ppermute | solution.py:13
  59.3 6.3 %copy-start.1 = (f32[384,384]{1,0:T(8,128)S(1)}, f32[384,384]{1,0:T(8,128)}, u32[]{:S(2)}) copy-start(f32[384,384]{1,0:T(8,128)} %all-reduce.7.cloned.1.call-done) | copy-start | bytes 1769476
  72.9 5.3 %collective-permute-start.2 = (bf16[384,192]{0,1:T(8,128)(2,1)S(1)}, bf16[384,192]{0,1:T(8,128)(2,1)S(1)}, u32[]{:S(2)}, u32[]{:S(2)}) collective-permute-start(bf16[384,192]{0,1:T(8,128)(2,1)S(1)} %get-tuple-element.12), channel_id=1, source_target_pairs={{0,7},{1,0},{2,1},{3,2},{4,3},{5,4},{6,5},{7,6},{8,15},{9,8},{10,9... | collective-permute-start | bytes 442376 | tf_op jit(solution)/shard_map/ppermute | solution.py:13
  75.4 6.4 %collective-permute-start = (bf16[384,192]{0,1:T(8,128)(2,1)S(1)}, bf16[384,192]{0,1:T(8,128)(2,1)S(1)}, u32[]{:S(2)}, u32[]{:S(2)}) collective-permute-start(bf16[384,192]{0,1:T(8,128)(2,1)S(1)} %get-tuple-element.11), channel_id=1, source_target_pairs={{0,1},{1,2},{2,3},{3,4},{4,5},{5,6},{6,7},{7,0},{8,9},{9,10},{10,1... | collective-permute-start | bytes 442376 | tf_op jit(solution)/shard_map/ppermute | solution.py:13
  87.0 62.7 %collective-permute-start.6 = (bf16[2048,384]{0,1:T(8,128)(2,1)}, bf16[2048,384]{0,1:T(8,128)(2,1)}, u32[]{:S(2)}, u32[]{:S(2)}) collective-permute-start(bf16[2048,384]{0,1:T(8,128)(2,1)} %pad_maximum_fusion), channel_id=1, source_target_pairs={{0,7},{1,0},{2,1},{3,2},{4,3},{5,4},{6,5},{7,6},{8,15},{9,8},{10,9... | collective-permute-start | bytes 4718600 | tf_op jit(solution)/shard_map/ppermute | solution.py:13
  89.3 64.1 %collective-permute-start.4 = (bf16[2048,384]{0,1:T(8,128)(2,1)}, bf16[2048,384]{0,1:T(8,128)(2,1)S(1)}, u32[]{:S(2)}, u32[]{:S(2)}) collective-permute-start(bf16[2048,384]{0,1:T(8,128)(2,1)} %pad_maximum_fusion), channel_id=1, source_target_pairs={{0,1},{1,2},{2,3},{3,4},{4,5},{5,6},{6,7},{7,0},{8,9},{9,10},{10,1... | collective-permute-start | bytes 4718600 | tf_op jit(solution)/shard_map/ppermute | solution.py:13
  130.9 6.4 %copy-start = (f32[384,384]{1,0:T(8,128)S(1)}, f32[384,384]{1,0:T(8,128)}, u32[]{:S(2)}) copy-start(f32[384,384]{1,0:T(8,128)} %all-reduce.9.cloned.1.call-done) | copy-start | bytes 1769476
  144.4 5.3 %collective-permute-start.7 = (bf16[384,192]{0,1:T(8,128)(2,1)S(1)}, bf16[384,192]{0,1:T(8,128)(2,1)S(1)}, u32[]{:S(2)}, u32[]{:S(2)}) collective-permute-start(bf16[384,192]{0,1:T(8,128)(2,1)S(1)} %get-tuple-element.10), channel_id=1, source_target_pairs={{0,7},{1,0},{2,1},{3,2},{4,3},{5,4},{6,5},{7,6},{8,15},{9,8},{10,9... | collective-permute-start | bytes 442376 | tf_op jit(solution)/shard_map/ppermute | solution.py:13
  147.0 6.4 %collective-permute-start.5 = (bf16[384,192]{0,1:T(8,128)(2,1)S(1)}, bf16[384,192]{0,1:T(8,128)(2,1)S(1)}, u32[]{:S(2)}, u32[]{:S(2)}) collective-permute-start(bf16[384,192]{0,1:T(8,128)(2,1)S(1)} %get-tuple-element.9), channel_id=1, source_target_pairs={{0,1},{1,2},{2,3},{3,4},{4,5},{5,6},{6,7},{7,0},{8,9},{9,10},{10,1... | collective-permute-start | bytes 442376 | tf_op jit(solution)/shard_map/ppermute | solution.py:13
Sparse Core Ops, SparseCore 0:
  10.6 48.6 all-reduce.6
  85.9 44.8 all-reduce.8
where the time goes:
time: 163 us; the launch traced here: 162 us
  waiting for transfers between devices  94.4 us (58%)
  matrix products  23.3 us (14%)
  between operations  15 us (9%)
  local copies, waits for them, and re-layouts  14.6 us (9%)
  starting transfers between devices  12 us (7%)
  other arithmetic  3.22 us (2%)
    psum x2, waiting for transfers between devices, rotor_of(): gram = lax.psum(gram, 'rows')  85.8 us
    gather x2, local copies, waits for them, and re-layouts, rotor_of(): return orthogonal(jnp.diagonal(gram), gram[:half, half:])  12.5 us
    ppermute x8, starting transfers between devices, passed_along(): lax.ppermute(shard, axis, [(i, (i + by) % peers) for i in range(peers)])  11.9 us
    ppermute x8, waiting for transfers between devices, passed_along(): lax.ppermute(shard, axis, [(i, (i + by) % peers) for i in range(peers)])  8.62 us
    dot_general x2, matrix products, rotor_of(): gram = jnp.dot(window.T, window, preferred_element_type=jnp.float32)  5.76 us
    dot_general x4, matrix products, orthogonal(): jnp.dot(current, inner, precision=lax.Precision.HIGHEST)  5.51 us
    dot_general x4, matrix products, orthogonal(): inner = jnp.dot(current.T, current, precision=lax.Precision.HIGHEST)  5.23 us
    dot_general x2, matrix products, local(): jnp.dot(from_above, right_rotor, preferred_element_type=jnp.float32)  4.1 us
  transfers between devices with their start and end apart: 10, of which 6 were waited for; matrix products, arithmetic and copies ran while one was open for 19% of the time, Pallas kernels for 0%

commit v1 on v0

--- a/solution.py
+++ b/solution.py
@@ -32,7 +32,7 @@
 def rotor_of(window):
     half = window.shape[1] // 2
     gram = jnp.dot(window.T, window, preferred_element_type=jnp.float32)
-    gram = lax.psum(gram, "rows")
+    gram = jnp.sum(lax.all_gather(gram, "rows"), axis=0)
     return orthogonal(jnp.diagonal(gram), gram[:half, half:])
 
 

time: 163 us -> 144 us (0.88)
  waiting for transfers between devices: 94.4 us -> 77.2 us
  local copies, waits for them, and re-layouts: 14.6 us -> 8.9 us
  other arithmetic: 3.22 us -> 6.99 us
    psum x2 -> x0, waiting for transfers between devices: 85.8 us -> none  [rotor_of(): gram = lax.psum(gram, 'rows')]
    all_gather x0 -> x2, waiting for transfers between devices: none -> 68.5 us  [rotor_of(): gram = jnp.sum(lax.all_gather(gram, 'rows'), axis=0)]
    gather x2, local copies, waits for them, and re-layouts: 12.5 us -> 6.89 us  [rotor_of(): return orthogonal(jnp.diagonal(gram), gram[:half, half:])]
    reduce_sum x0 -> x2, other arithmetic: none -> 3.75 us  [rotor_of(): gram = jnp.sum(lax.all_gather(gram, 'rows'), axis=0)]
  transfers between devices with their start and end apart: 10 -> 10, of which waited for: 6 -> 6; matrix products, arithmetic and copies ran while one was open for 19% -> 20% of each run, Pallas kernels for 0% -> 0%
where the time goes in v1:
time: 144 us; the launch traced here: 143 us
  waiting for transfers between devices  77.2 us (54%)
  matrix products  23.2 us (16%)
  between operations  15 us (10%)
  starting transfers between devices  12.1 us (8%)
  local copies, waits for them, and re-layouts  8.9 us (6%)
  other arithmetic  6.99 us (5%)
    all_gather x2, waiting for transfers between devices, rotor_of(): gram = jnp.sum(lax.all_gather(gram, 'rows'), axis=0)  68.5 us
    ppermute x8, starting transfers between devices, passed_along(): lax.ppermute(shard, axis, [(i, (i + by) % peers) for i in range(peers)])  12 us
    ppermute x8, waiting for transfers between devices, passed_along(): lax.ppermute(shard, axis, [(i, (i + by) % peers) for i in range(peers)])  8.6 us
    gather x2, local copies, waits for them, and re-layouts, rotor_of(): return orthogonal(jnp.diagonal(gram), gram[:half, half:])  6.89 us
    dot_general x2, matrix products, rotor_of(): gram = jnp.dot(window.T, window, preferred_element_type=jnp.float32)  5.68 us
    dot_general x4, matrix products, orthogonal(): jnp.dot(current, inner, precision=lax.Precision.HIGHEST)  5.51 us
    dot_general x4, matrix products, orthogonal(): inner = jnp.dot(current.T, current, precision=lax.Precision.HIGHEST)  5.22 us
    dot_general x2, matrix products, local(): jnp.dot(from_above, right_rotor, preferred_element_type=jnp.float32)  4.09 us
  transfers between devices with their start and end apart: 10, of which 6 were waited for; matrix products, arithmetic and copies ran while one was open for 20% of the time, Pallas kernels for 0%

profile of v1, /device:TPU:0, one launch (start us, length us, event | category | flops | bytes accessed | tf_op | source)
XLA Modules:
  0.0 143.3 jit_solution(10437077955305244907)
XLA Ops:
  6.5 3.9 %fusion.51 = f32[384,384]{1,0:T(8,128)} fusion(bf16[2048,384]{1,0:T(8,128)(2,1)} %param.1), kind=kOutput, calls=%fused_computation.75 | convolution fusion | flops 603979776 | bytes 2162688 | tf_op jit(solution)/shard_map/dot_general | solution.py:34
  10.5 4.6 %collective-permute-start.3 = (bf16[2048,384]{1,0:T(8,128)(2,1)S(1)}, bf16[2048,384]{1,0:T(8,128)(2,1)}, u32[]{:S(2)}, u32[]{:S(2)}) collective-permute-start(bf16[2048,384]{1,0:T(8,128)(2,1)S(1)} %copy-done), channel_id=1, source_target_pairs={{0,7},{1,0},{2,1},{3,2},{4,3},{5,4},{6,5},{7,6},{8,15},{9,8},{10,9... | collective-permute-start | bytes 4718600 | tf_op jit(solution)/shard_map/ppermute | solution.py:13
  15.1 35.6 %all-gather.5.cloned.1.call-done = f32[1536,384]{1,0:T(8,128)} async-done(((f32[384,384]{1,0:T(8,128)}), f32[1536,384]{1,0:T(8,128)}) %all-gather.5.cloned.1.call-update) | async-done | bytes 2359312 | tf_op jit(solution)/shard_map/all_gather | solution.py:35
  50.7 1.9 %reduce_sum.36 = f32[384,384]{1,0:T(8,128)S(1)} reduce(f32[4,384,384]{2,1,0:T(8,128)} %bitcast.31, f32[]{:T(128)} %constant.8.clone.1), dimensions={0}, to_apply=%region_0.0 | reduce | flops 442368 | bytes 2949124 | tf_op jit(solution)/shard_map/reduce_sum | solution.py:35
  52.6 3.4 %gather_fusion = f32[384]{0:T(512)S(1)} fusion(f32[384,384]{1,0:T(8,128)S(1)} %reduce_sum.36, s32[384]{0:T(512)S(1)} %or_reduce_fusion), kind=kCustom, calls=%fused_computation | custom fusion | bytes 6144 | tf_op jit(solution)/shard_map/jit(diagonal)/cond/branch_0_fun/gather | solution.py:36
  57.8 1.3 fusion.12
  59.1 1.4 %fusion.2 = f32[384,384]{0,1:T(8,128)S(1)} fusion(f32[384,384]{1,0:T(8,128)S(1)} %fusion.12, f32[192,192]{0,1:T(8,128)S(1)} %get-tuple-element.7, f32[192,192]{0,1:T(8,128)S(1)} %copy.8), kind=kOutput, calls=%fused_computation.14 | convolution fusion | flops 682426368 | bytes 1474560 | tf_op jit(solution)/shard_map/dot_general | solution.py:28
  61.9 1.3 fusion.7
  63.3 2.6 %collective-permute-start.2 = (bf16[384,192]{0,1:T(8,128)(2,1)S(1)}, bf16[384,192]{0,1:T(8,128)(2,1)S(1)}, u32[]{:S(2)}, u32[]{:S(2)}) collective-permute-start(bf16[384,192]{0,1:T(8,128)(2,1)S(1)} %get-tuple-element.12), channel_id=1, source_target_pairs={{0,7},{1,0},{2,1},{3,2},{4,3},{5,4},{6,5},{7,6},{8,15},{9,8},{10,9... | collective-permute-start | bytes 442376 | tf_op jit(solution)/shard_map/ppermute | solution.py:13
  65.9 2.7 %collective-permute-done.2 = bf16[384,192]{0,1:T(8,128)(2,1)S(1)} collective-permute-done((bf16[384,192]{0,1:T(8,128)(2,1)S(1)}, bf16[384,192]{0,1:T(8,128)(2,1)S(1)}, u32[]{:S(2)}, u32[]{:S(2)}) %collective-permute-start.2) | collective-permute-done | bytes 147488 | tf_op jit(solution)/shard_map/ppermute | solution.py:13
  68.6 2.1 %fusion.1 = bf16[2048,192]{0,1:T(8,128)(2,1)S(1)} fusion(bf16[384,192]{0,1:T(8,128)(2,1)S(1)} %collective-permute-done.2, bf16[2048,384]{1,0:T(8,128)(2,1)} %collective-permute-done.3), kind=kOutput, calls=%fused_computation.7 | convolution fusion | flops 302383104 | bytes 2506752 | tf_op jit(solution)/shard_map/dot_general | solution.py:51
  70.7 1.6 %collective-permute-done = bf16[384,192]{0,1:T(8,128)(2,1)S(1)} collective-permute-done((bf16[384,192]{0,1:T(8,128)(2,1)S(1)}, bf16[384,192]{0,1:T(8,128)(2,1)S(1)}, u32[]{:S(2)}, u32[]{:S(2)}) %collective-permute-start) | collective-permute-done | bytes 147488 | tf_op jit(solution)/shard_map/ppermute | solution.py:13
  72.3 2.1 %fusion = bf16[2048,192]{0,1:T(8,128)(2,1)S(1)} fusion(bf16[384,192]{0,1:T(8,128)(2,1)S(1)} %collective-permute-done, bf16[2048,384]{1,0:T(8,128)(2,1)} %collective-permute-done.1), kind=kOutput, calls=%fused_computation.6 | convolution fusion | flops 302383104 | bytes 2506752 | tf_op jit(solution)/shard_map/dot_general | solution.py:48
  74.4 1.8 %fusion.44 = f32[384,384]{1,0:T(8,128)} fusion(bf16[2048,192]{0,1:T(8,128)(2,1)S(1)} %fusion.1, bf16[2048,192]{0,1:T(8,128)(2,1)S(1)} %fusion), kind=kOutput, calls=%fused_computation.70 | convolution fusion | flops 607125504 | bytes 2162688 | tf_op jit(solution)/shard_map/dot_general | solution.py:34
  77.5 2.1 %collective-permute-start.6 = (bf16[2048,384]{0,1:T(8,128)(2,1)}, bf16[2048,384]{0,1:T(8,128)(2,1)}, u32[]{:S(2)}, u32[]{:S(2)}) collective-permute-start(bf16[2048,384]{0,1:T(8,128)(2,1)} %pad_maximum_fusion), channel_id=1, source_target_pairs={{0,7},{1,0},{2,1},{3,2},{4,3},{5,4},{6,5},{7,6},{8,15},{9,8},{10,9... | collective-permute-start | bytes 4718600 | tf_op jit(solution)/shard_map/ppermute | solution.py:13
  79.6 33.0 %all-gather.7.cloned.1.call-done = f32[1536,384]{1,0:T(8,128)} async-done(((f32[384,384]{1,0:T(8,128)}), f32[1536,384]{1,0:T(8,128)}) %all-gather.7.cloned.1.call-update) | async-done | bytes 2359312 | tf_op jit(solution)/shard_map/all_gather | solution.py:35
  112.6 1.9 %reduce_sum.38 = f32[384,384]{1,0:T(8,128)S(1)} reduce(f32[4,384,384]{2,1,0:T(8,128)} %bitcast.30, f32[]{:T(128)} %constant.8.clone.1), dimensions={0}, to_apply=%region_2.3 | reduce | flops 442368 | bytes 2949124 | tf_op jit(solution)/shard_map/reduce_sum | solution.py:35
  114.4 3.4 %gather_fusion.1 = f32[384]{0:T(512)S(1)} fusion(f32[384,384]{1,0:T(8,128)S(1)} %reduce_sum.38, s32[384]{0:T(512)S(1)} %or_reduce_fusion), kind=kCustom, calls=%fused_computation.1 | custom fusion | bytes 6144 | tf_op jit(solution)/shard_map/jit(diagonal)/cond/branch_0_fun/gather | solution.py:36
  121.2 1.4 fusion.4
  125.2 2.7 %collective-permute-start.7 = (bf16[384,192]{0,1:T(8,128)(2,1)S(1)}, bf16[384,192]{0,1:T(8,128)(2,1)S(1)}, u32[]{:S(2)}, u32[]{:S(2)}) collective-permute-start(bf16[384,192]{0,1:T(8,128)(2,1)S(1)} %get-tuple-element.10), channel_id=1, source_target_pairs={{0,7},{1,0},{2,1},{3,2},{4,3},{5,4},{6,5},{7,6},{8,15},{9,8},{10,9... | collective-permute-start | bytes 442376 | tf_op jit(solution)/shard_map/ppermute | solution.py:13
  127.9 2.7 %collective-permute-done.7 = bf16[384,192]{0,1:T(8,128)(2,1)S(1)} collective-permute-done((bf16[384,192]{0,1:T(8,128)(2,1)S(1)}, bf16[384,192]{0,1:T(8,128)(2,1)S(1)}, u32[]{:S(2)}, u32[]{:S(2)}) %collective-permute-start.7) | collective-permute-done | bytes 147488 | tf_op jit(solution)/shard_map/ppermute | solution.py:13
  130.5 2.0 %convolution_convert_fusion = bf16[2048,192]{0,1:T(8,128)(2,1)S(1)} fusion(bf16[384,192]{0,1:T(8,128)(2,1)S(1)} %collective-permute-done.7, bf16[2048,384]{0,1:T(8,128)(2,1)} %collective-permute-done.6), kind=kOutput, calls=%fused_computation.2 | convolution fusion | flops 302383104 | bytes 2506752 | tf_op jit(solution)/shard_map/dot_general | solution.py:51
  132.5 1.7 %collective-permute-done.5 = bf16[384,192]{0,1:T(8,128)(2,1)S(1)} collective-permute-done((bf16[384,192]{0,1:T(8,128)(2,1)S(1)}, bf16[384,192]{0,1:T(8,128)(2,1)S(1)}, u32[]{:S(2)}, u32[]{:S(2)}) %collective-permute-start.5) | collective-permute-done | bytes 147488 | tf_op jit(solution)/shard_map/ppermute | solution.py:13
  134.9 1.6 %copy.7 = bf16[2048,384]{1,0:T(8,128)(2,1)} copy(bf16[2048,384]{0,1:T(8,128)(2,1)S(1)} %pad_maximum_fusion.1) | data formatting | bytes 3145728 | tf_op jit(solution)/shard_map/concatenate | solution.py:54
  (32 shorter events, 9.6 us)
Async XLA Ops:
  6.5 4.0 %copy-start = (bf16[2048,384]{1,0:T(8,128)(2,1)S(1)}, bf16[2048,384]{1,0:T(8,128)(2,1)}, u32[]{:S(2)}) copy-start(bf16[2048,384]{1,0:T(8,128)(2,1)} %param.1) | copy-start | bytes 4718596
  6.5 44.1 %all-gather.5.cloned.1.call-start = ((), (), s32[]{:S(2)}) async-start(), calls=%async_computation | async-start | bytes 2949120 | tf_op jit(solution)/shard_map/all_gather | solution.py:35
  10.4 102.1 %all-gather.7.cloned.1.call-start = ((), (), s32[]{:S(2)}) async-start(), calls=%async_computation.1 | async-start | bytes 2949120 | tf_op jit(solution)/shard_map/all_gather | solution.py:35
  10.5 55.4 %collective-permute-start.3 = (bf16[2048,384]{1,0:T(8,128)(2,1)S(1)}, bf16[2048,384]{1,0:T(8,128)(2,1)}, u32[]{:S(2)}, u32[]{:S(2)}) collective-permute-start(bf16[2048,384]{1,0:T(8,128)(2,1)S(1)} %copy-done), channel_id=1, source_target_pairs={{0,7},{1,0},{2,1},{3,2},{4,3},{5,4},{6,5},{7,6},{8,15},{9,8},{10,9... | collective-permute-start | bytes 4718600 | tf_op jit(solution)/shard_map/ppermute | solution.py:13
  15.1 55.6 %collective-permute-start.1 = (bf16[2048,384]{1,0:T(8,128)(2,1)S(1)}, bf16[2048,384]{1,0:T(8,128)(2,1)}, u32[]{:S(2)}, u32[]{:S(2)}) collective-permute-start(bf16[2048,384]{1,0:T(8,128)(2,1)S(1)} %copy-done), channel_id=1, source_target_pairs={{0,1},{1,2},{2,3},{3,4},{4,5},{5,6},{6,7},{7,0},{8,9},{9,10},{10,1... | collective-permute-start | bytes 4718600 | tf_op jit(solution)/shard_map/ppermute | solution.py:13
  63.3 5.3 %collective-permute-start.2 = (bf16[384,192]{0,1:T(8,128)(2,1)S(1)}, bf16[384,192]{0,1:T(8,128)(2,1)S(1)}, u32[]{:S(2)}, u32[]{:S(2)}) collective-permute-start(bf16[384,192]{0,1:T(8,128)(2,1)S(1)} %get-tuple-element.12), channel_id=1, source_target_pairs={{0,7},{1,0},{2,1},{3,2},{4,3},{5,4},{6,5},{7,6},{8,15},{9,8},{10,9... | collective-permute-start | bytes 442376 | tf_op jit(solution)/shard_map/ppermute | solution.py:13
  65.9 6.4 %collective-permute-start = (bf16[384,192]{0,1:T(8,128)(2,1)S(1)}, bf16[384,192]{0,1:T(8,128)(2,1)S(1)}, u32[]{:S(2)}, u32[]{:S(2)}) collective-permute-start(bf16[384,192]{0,1:T(8,128)(2,1)S(1)} %get-tuple-element.11), channel_id=1, source_target_pairs={{0,1},{1,2},{2,3},{3,4},{4,5},{5,6},{6,7},{7,0},{8,9},{9,10},{10,1... | collective-permute-start | bytes 442376 | tf_op jit(solution)/shard_map/ppermute | solution.py:13
  77.5 50.4 %collective-permute-start.6 = (bf16[2048,384]{0,1:T(8,128)(2,1)}, bf16[2048,384]{0,1:T(8,128)(2,1)}, u32[]{:S(2)}, u32[]{:S(2)}) collective-permute-start(bf16[2048,384]{0,1:T(8,128)(2,1)} %pad_maximum_fusion), channel_id=1, source_target_pairs={{0,7},{1,0},{2,1},{3,2},{4,3},{5,4},{6,5},{7,6},{8,15},{9,8},{10,9... | collective-permute-start | bytes 4718600 | tf_op jit(solution)/shard_map/ppermute | solution.py:13
  79.6 52.9 %collective-permute-start.4 = (bf16[2048,384]{0,1:T(8,128)(2,1)}, bf16[2048,384]{0,1:T(8,128)(2,1)S(1)}, u32[]{:S(2)}, u32[]{:S(2)}) collective-permute-start(bf16[2048,384]{0,1:T(8,128)(2,1)} %pad_maximum_fusion), channel_id=1, source_target_pairs={{0,1},{1,2},{2,3},{3,4},{4,5},{5,6},{6,7},{7,0},{8,9},{9,10},{10,1... | collective-permute-start | bytes 4718600 | tf_op jit(solution)/shard_map/ppermute | solution.py:13
  125.2 5.3 %collective-permute-start.7 = (bf16[384,192]{0,1:T(8,128)(2,1)S(1)}, bf16[384,192]{0,1:T(8,128)(2,1)S(1)}, u32[]{:S(2)}, u32[]{:S(2)}) collective-permute-start(bf16[384,192]{0,1:T(8,128)(2,1)S(1)} %get-tuple-element.10), channel_id=1, source_target_pairs={{0,7},{1,0},{2,1},{3,2},{4,3},{5,4},{6,5},{7,6},{8,15},{9,8},{10,9... | collective-permute-start | bytes 442376 | tf_op jit(solution)/shard_map/ppermute | solution.py:13
  127.9 6.4 %collective-permute-start.5 = (bf16[384,192]{0,1:T(8,128)(2,1)S(1)}, bf16[384,192]{0,1:T(8,128)(2,1)S(1)}, u32[]{:S(2)}, u32[]{:S(2)}) collective-permute-start(bf16[384,192]{0,1:T(8,128)(2,1)S(1)} %get-tuple-element.9), channel_id=1, source_target_pairs={{0,1},{1,2},{2,3},{3,4},{4,5},{5,6},{6,7},{7,0},{8,9},{9,10},{10,1... | collective-permute-start | bytes 442376 | tf_op jit(solution)/shard_map/ppermute | solution.py:13
Sparse Core Ops, SparseCore 0:
  10.6 40.0 all-gather.4
  76.3 36.1 all-gather.6
